TPU v7x, 32 devices: a whole 2x2x4 slice. The times are simulated.
32 devices in a mesh: wide: 8 (over z, x), narrow: 4 (over y, core).
Axes of the slice: x: 2, y: 2, z: 4, core: 2. Of those that a mesh axis runs over, the one named last changes fastest.
Arguments:
- hidden_in: bfloat16 [16384, 1024], P(('wide', 'narrow')), may hold values from -6 to 6
- grad_out: bfloat16 [16384, 1024], P(('wide', 'narrow')), may hold values from -6 to 6
- gain_attn: bfloat16 [1024], replicated, may hold values from 0.5 to 1.5
- gain_ffn: bfloat16 [1024], replicated, may hold values from 0.5 to 1.5
- w_query: bfloat16 [1024, 1024], P(None, 'narrow'), may hold values from -0.046875 to 0.046875
- w_key: bfloat16 [1024, 1024], P(None, 'narrow'), may hold values from -0.1875 to 0.1875
- w_value: bfloat16 [1024, 1024], P(None, 'narrow'), may hold values from -0.1875 to 0.1875
- w_output: bfloat16 [1024, 1024], P('narrow'), may hold values from -0.75 to 0.75
- table_rel: bfloat16 [32, 16], P(None, 'narrow'), may hold values from -4 to 4
- table_horiz: bfloat16 [32, 16], P(None, 'narrow'), may hold values from -4 to 4
- table_vert: bfloat16 [32, 16], P(None, 'narrow'), may hold values from -4 to 4
- wi_gate: bfloat16 [1024, 2816], P(None, 'narrow'), may hold values from -0.1875 to 0.1875
- wi_up: bfloat16 [1024, 2816], P(None, 'narrow'), may hold values from -0.1875 to 0.1875
- wo_ffn: bfloat16 [2816, 1024], P('narrow'), may hold values from -0.21875 to 0.21875
- counts: int32 [32], P('wide'), may hold values from 1 to 256
- patch_mask: int32 [32, 256], P('wide'), may hold values 0 or 1
- bucket_rel: int32 [32, 512, 512], P('wide'), may hold values from 0 to 31
- bucket_horiz: int32 [32, 512, 512], P('wide'), may hold values from 0 to 31
- bucket_vert: int32 [32, 512, 512], P('wide'), may hold values from 0 to 31
Outputs:
- block_out: bfloat16 [16384, 1024], P(('wide', 'narrow'))
- grad_input: float32 [16384, 1024], P(('wide', 'narrow'))
- grad_gain_attn: float32 [1024], P(('wide', 'narrow'))
- grad_gain_ffn: float32 [1024], P(('wide', 'narrow'))
- grad_w_query: float32 [1024, 1024], P('wide', 'narrow')
- grad_w_key: float32 [1024, 1024], P('wide', 'narrow')
- grad_w_value: float32 [1024, 1024], P('wide', 'narrow')
- grad_w_output: float32 [1024, 1024], P('narrow', 'wide')
- grad_table_rel: float32 [32, 16], P('wide', 'narrow')
- grad_table_horiz: float32 [32, 16], P('wide', 'narrow')
- grad_table_vert: float32 [32, 16], P('wide', 'narrow')
- grad_wi_gate: float32 [1024, 2816], P('wide', 'narrow')
- grad_wi_up: float32 [1024, 2816], P('wide', 'narrow')
- grad_wo_ffn: float32 [2816, 1024], P('narrow', 'wide')
All inputs are finite; a program needn't handle non-finite values. No bound on the sum of `patch_mask` on one device may be relied on, other than what follows from the above.
Results may differ from a plain program's by a relative error of at most 0.02.
Values may be sent and summed in bfloat16 or wider, within the bound.
A program may use at most 256 MiB of HBM per device.

v0:
```python
from functools import partial
import jax
import jax.numpy as jnp
from jax import lax
from jax.sharding import PartitionSpec as P

HEAD_DIM = 64
EPS = 1e-06
MASKED = -1000000000.0


def rms_forward(row_data, gain_vec):
    inv_rms = lax.rsqrt(jnp.mean(row_data * row_data, axis=-1, keepdims=True) + EPS)
    return (row_data * inv_rms * gain_vec, inv_rms)


def rms_backward(upstream, row_data, inv_rms, gain_vec):
    lifted = upstream * gain_vec
    inner = jnp.mean(lifted * row_data, axis=-1, keepdims=True)
    grad_rows = inv_rms * lifted - row_data * inv_rms * inv_rms * inv_rms * inner
    grad_gain = jnp.sum(upstream * row_data * inv_rms, axis=0)
    return (grad_rows, grad_gain)


def bucket_onehot(bucket_rel, bucket_horiz, bucket_vert, buckets):
    levels = jnp.arange(buckets, dtype=jnp.int32)[None, :, None]
    pieces = [
        (bucket_ids[:, None, :] == levels).astype(jnp.bfloat16)
        for bucket_ids in (bucket_rel, bucket_horiz, bucket_vert)
    ]
    return jnp.concatenate(pieces, axis=1)


def page_scores(queries, key_rows, one_hot, table_all, valid):
    scores = jnp.einsum("ihd,jhd->hij", queries, key_rows, preferred_element_type=jnp.float32)
    scores = scores + jnp.einsum(
        "ibj,bh->hij", one_hot, table_all, preferred_element_type=jnp.float32
    )
    return jnp.where(valid[None, None, :], scores, MASKED)


def page_forward(table_all, page_data):
    queries, key_rows, values, bucket_rel, bucket_horiz, bucket_vert, valid = page_data
    one_hot = bucket_onehot(bucket_rel, bucket_horiz, bucket_vert, table_all.shape[0] // 3)
    scores = page_scores(queries, key_rows, one_hot, table_all, valid)
    peak = jnp.max(scores, axis=-1, keepdims=True)
    raised = jnp.exp(scores - peak)
    summed = jnp.sum(raised, axis=-1, keepdims=True)
    weights_low = (raised / summed).astype(jnp.bfloat16)
    context = jnp.einsum("hij,jhd->ihd", weights_low, values, preferred_element_type=jnp.float32)
    return (context.astype(jnp.bfloat16), (peak + jnp.log(summed))[..., 0])


def page_backward(table_all, page_data):
    (
        queries,
        key_rows,
        values,
        grad_context,
        bucket_rel,
        bucket_horiz,
        bucket_vert,
        valid,
        log_total,
    ) = page_data
    one_hot = bucket_onehot(bucket_rel, bucket_horiz, bucket_vert, table_all.shape[0] // 3)
    scores = page_scores(queries, key_rows, one_hot, table_all, valid)
    weights = jnp.exp(scores - log_total[..., None])
    weights_low = weights.astype(jnp.bfloat16)
    grad_values = jnp.einsum(
        "hij,ihd->jhd", weights_low, grad_context, preferred_element_type=jnp.float32
    )
    grad_weights = jnp.einsum(
        "ihd,jhd->hij", grad_context, values, preferred_element_type=jnp.float32
    )
    grad_scores = weights * (grad_weights - jnp.sum(weights * grad_weights, axis=-1, keepdims=True))
    grad_low = grad_scores.astype(jnp.bfloat16)
    grad_queries = jnp.einsum(
        "hij,jhd->ihd", grad_low, key_rows, preferred_element_type=jnp.float32
    )
    grad_keys = jnp.einsum("hij,ihd->jhd", grad_low, queries, preferred_element_type=jnp.float32)
    grad_table = jnp.einsum("ibj,hij->bh", one_hot, grad_low, preferred_element_type=jnp.float32)
    return (
        grad_queries.astype(jnp.bfloat16),
        grad_keys.astype(jnp.bfloat16),
        grad_values.astype(jnp.bfloat16),
        grad_table,
    )


def gated(gate, upper):
    return jax.nn.gelu(gate, approximate=True) * upper


def shards(
    hidden_in,
    grad_out,
    gain_attn,
    gain_ffn,
    w_query,
    w_key,
    w_value,
    w_output,
    table_rel,
    table_horiz,
    table_vert,
    wi_gate,
    wi_up,
    wo_ffn,
    counts,
    patch_mask,
    bucket_rel,
    bucket_horiz,
    bucket_vert,
):
    page_count = bucket_rel.shape[0]
    slot_count = bucket_rel.shape[1]
    local_heads = table_rel.shape[1]
    local_width = w_query.shape[1]
    group_rows = page_count * slot_count
    bucket_count = table_rel.shape[0]
    positions = jnp.arange(slot_count, dtype=jnp.int32)
    text_length = slot_count - patch_mask.shape[1]
    valid = jnp.concatenate(
        [positions[None, :text_length] < counts[:, None], patch_mask == 1], axis=1
    )
    table_all = jnp.concatenate([table_rel, table_horiz, table_vert], axis=0)
    w_joined = jnp.concatenate([w_query, w_key, w_value], axis=1)
    gain_first = gain_attn.astype(jnp.float32)
    gain_second = gain_ffn.astype(jnp.float32)
    resid = hidden_in.astype(jnp.float32)
    normed, inv_first = rms_forward(resid, gain_first)
    normed_all = lax.all_gather(normed.astype(jnp.bfloat16), "narrow", axis=0, tiled=True)
    projected = jnp.dot(normed_all, w_joined, preferred_element_type=jnp.float32).astype(
        jnp.bfloat16
    )
    shaped = projected.reshape(page_count, slot_count, 3, local_heads, HEAD_DIM)
    queries = shaped[:, :, 0]
    key_rows = shaped[:, :, 1]
    values = shaped[:, :, 2]
    context, log_total = lax.map(
        partial(page_forward, table_all),
        (queries, key_rows, values, bucket_rel, bucket_horiz, bucket_vert, valid),
    )
    context_flat = context.reshape(group_rows, local_width)
    middle = resid + lax.psum_scatter(
        jnp.dot(context_flat, w_output, preferred_element_type=jnp.float32),
        "narrow",
        scatter_dimension=0,
        tiled=True,
    )
    normed_ffn, inv_second = rms_forward(middle, gain_second)
    normed_low = normed_ffn.astype(jnp.bfloat16)
    ffn_rows_all = lax.all_gather(normed_low, "narrow", axis=0, tiled=True)
    gate = jnp.dot(ffn_rows_all, wi_gate, preferred_element_type=jnp.float32)
    upper = jnp.dot(ffn_rows_all, wi_up, preferred_element_type=jnp.float32)
    hidden = gated(gate, upper).astype(jnp.bfloat16)
    ffn_out = lax.psum_scatter(
        jnp.dot(hidden, wo_ffn, preferred_element_type=jnp.float32).astype(jnp.bfloat16),
        "narrow",
        scatter_dimension=0,
        tiled=True,
    ).astype(jnp.float32)
    block_out = (middle + ffn_out).astype(jnp.bfloat16)
    grad_resid = grad_out.astype(jnp.float32)
    grad_all = lax.all_gather(grad_out, "narrow", axis=0, tiled=True)
    grad_hidden = jnp.dot(grad_all, wo_ffn.T, preferred_element_type=jnp.float32)
    grad_wo_ffn = jnp.dot(hidden.T, grad_all, preferred_element_type=jnp.float32)
    gated_out, pull = jax.vjp(gated, gate, upper)
    grad_gate, grad_upper = pull(grad_hidden)
    grad_gate = grad_gate.astype(jnp.bfloat16)
    grad_upper = grad_upper.astype(jnp.bfloat16)
    grad_wi_gate = jnp.dot(ffn_rows_all.T, grad_gate, preferred_element_type=jnp.float32)
    grad_wi_up = jnp.dot(ffn_rows_all.T, grad_upper, preferred_element_type=jnp.float32)
    first = jnp.dot(grad_gate, wi_gate.T, preferred_element_type=jnp.float32)
    grad_normed_ffn = lax.psum_scatter(
        first + jnp.dot(grad_upper, wi_up.T, preferred_element_type=jnp.float32),
        "narrow",
        scatter_dimension=0,
        tiled=True,
    )
    grad_middle_norm, grad_gain_second = rms_backward(
        grad_normed_ffn, middle, inv_second, gain_second
    )
    grad_middle = grad_resid + grad_middle_norm
    grad_attn_all = lax.all_gather(grad_middle.astype(jnp.bfloat16), "narrow", axis=0, tiled=True)
    grad_context = jnp.dot(grad_attn_all, w_output.T, preferred_element_type=jnp.float32).astype(
        jnp.bfloat16
    )
    grad_w_output = jnp.dot(context_flat.T, grad_attn_all, preferred_element_type=jnp.float32)
    grad_context_pages = grad_context.reshape(page_count, slot_count, local_heads, HEAD_DIM)
    grad_queries, grad_keys, grad_values, grad_tables = lax.map(
        partial(page_backward, table_all),
        (
            queries,
            key_rows,
            values,
            grad_context_pages,
            bucket_rel,
            bucket_horiz,
            bucket_vert,
            valid,
            log_total,
        ),
    )
    grad_table_all = jnp.sum(grad_tables, axis=0)
    grad_joined = jnp.stack([grad_queries, grad_keys, grad_values], axis=2).reshape(
        group_rows, 3 * local_width
    )
    grad_w_joined = jnp.dot(normed_all.T, grad_joined, preferred_element_type=jnp.float32)
    grad_normed = lax.psum_scatter(
        jnp.dot(grad_joined, w_joined.T, preferred_element_type=jnp.float32).astype(jnp.bfloat16),
        "narrow",
        scatter_dimension=0,
        tiled=True,
    ).astype(jnp.float32)
    grad_resid_norm, grad_gain_first = rms_backward(grad_normed, resid, inv_first, gain_first)
    grad_input = grad_middle + grad_resid_norm
    summed = (
        lax.psum_scatter(
            grad_w_joined[:, :local_width].astype(jnp.bfloat16),
            "wide",
            scatter_dimension=0,
            tiled=True,
        ).astype(jnp.float32),
        lax.psum_scatter(
            grad_w_joined[:, local_width : 2 * local_width].astype(jnp.bfloat16),
            "wide",
            scatter_dimension=0,
            tiled=True,
        ).astype(jnp.float32),
        lax.psum_scatter(
            grad_w_joined[:, 2 * local_width :].astype(jnp.bfloat16),
            "wide",
            scatter_dimension=0,
            tiled=True,
        ).astype(jnp.float32),
        lax.psum_scatter(
            grad_w_output.astype(jnp.bfloat16), "wide", scatter_dimension=1, tiled=True
        ).astype(jnp.float32),
        lax.psum_scatter(
            grad_table_all[:bucket_count].astype(jnp.bfloat16),
            "wide",
            scatter_dimension=0,
            tiled=True,
        ).astype(jnp.float32),
        lax.psum_scatter(
            grad_table_all[bucket_count : 2 * bucket_count].astype(jnp.bfloat16),
            "wide",
            scatter_dimension=0,
            tiled=True,
        ).astype(jnp.float32),
        lax.psum_scatter(
            grad_table_all[2 * bucket_count :].astype(jnp.bfloat16),
            "wide",
            scatter_dimension=0,
            tiled=True,
        ).astype(jnp.float32),
        lax.psum_scatter(
            grad_wi_gate.astype(jnp.bfloat16), "wide", scatter_dimension=0, tiled=True
        ).astype(jnp.float32),
        lax.psum_scatter(
            grad_wi_up.astype(jnp.bfloat16), "wide", scatter_dimension=0, tiled=True
        ).astype(jnp.float32),
        lax.psum_scatter(
            grad_wo_ffn.astype(jnp.bfloat16), "wide", scatter_dimension=1, tiled=True
        ).astype(jnp.float32),
    )
    gain_grads = (
        lax.psum_scatter(grad_gain_first, ("wide", "narrow"), scatter_dimension=0, tiled=True),
        lax.psum_scatter(grad_gain_second, ("wide", "narrow"), scatter_dimension=0, tiled=True),
    )
    return (
        block_out,
        grad_input,
        gain_grads[0],
        gain_grads[1],
        summed[0],
        summed[1],
        summed[2],
        summed[3],
        summed[4],
        summed[5],
        summed[6],
        summed[7],
        summed[8],
        summed[9],
    )


def solution(mesh):
    return jax.shard_map(
        shards,
        mesh=mesh,
        in_specs=(
            P(("wide", "narrow"), None),
            P(("wide", "narrow"), None),
            P(),
            P(),
            P(None, "narrow"),
            P(None, "narrow"),
            P(None, "narrow"),
            P("narrow", None),
            P(None, "narrow"),
            P(None, "narrow"),
            P(None, "narrow"),
            P(None, "narrow"),
            P(None, "narrow"),
            P("narrow", None),
            P("wide"),
            P("wide", None),
            P("wide", None, None),
            P("wide", None, None),
            P("wide", None, None),
        ),
        out_specs=(
            P(("wide", "narrow"), None),
            P(("wide", "narrow"), None),
            P(("wide", "narrow")),
            P(("wide", "narrow")),
            P("wide", "narrow"),
            P("wide", "narrow"),
            P("wide", "narrow"),
            P("narrow", "wide"),
            P("wide", "narrow"),
            P("wide", "narrow"),
            P("wide", "narrow"),
            P("wide", "narrow"),
            P("wide", "narrow"),
            P("narrow", "wide"),
        ),
        check_vma=False,
    )
```

profile of v0, /device:TPU:0, one launch (start us, length us, event | category | flops | bytes accessed | tf_op | source)
XLA Modules:
  0.0 1441.9 jit_solution(14907806034434537034)
XLA Ops:
  15.8 34.4 %all-gather.5.cloned.1.call-done = bf16[2048,1024]{1,0:T(8,128)(2,1)} async-done(((bf16[512,1024]{1,0:T(8,128)(2,1)}), bf16[2048,1024]{1,0:T(8,128)(2,1)}) %all-gather.5.cloned.1.call-update) | async-done | bytes 4194320 | tf_op jit(solution)/shard_map/all_gather | solution.py:133
  76.8 243.5 %while.28 = (s32[]{:T(128)}, bf16[4,512,4,64]{1,3,2,0:T(8,128)(2,1)}, f32[4,4,512]{2,1,0:T(4,128)}, bf16[4,512,4,64]{1,3,2,0:T(8,128)(2,1)}, pred[4,512]{1,0:T(4...) while((s32[]{:T(128)}, ...), condition=%wide.region_4.5_spmd, body=%wide.region_1.4_spmd.sunk | while | flops 553777152 | bytes 90247560 | solution.py:141
  108.1 17.5 %fusion.146 = f32[512,512,4]{1,2,0:T(4,128)} fusion(pred[512,32,512]{2,1,0:T(32,128)(4,1)} %iota_compare_fusion.12, pred[512,32,512]{2,1,0:T(32,128)(4,1)} %iota_compare_fusion.13, pred[512,32,512]{2,1,0:T(32,128)(4,1)} %iota_compare_fusion.14, bf16[96,4]{0,1:T(4,128)(2,1)S(1)} %get-tuple-element.520), kind=kOutput, calls=%fused_computation.1.clone.1 | convolution fusion | flops 251658240 | bytes 29360896 | tf_op jit(solution)/shard_map/while/body/eval_jaxpr/ibj,bh->hij/dot_general | solution.py:36
  168.8 17.5 %fusion.146 = f32[512,512,4]{1,2,0:T(4,128)} fusion(pred[512,32,512]{2,1,0:T(32,128)(4,1)} %iota_compare_fusion.12, pred[512,32,512]{2,1,0:T(32,128)(4,1)} %iota_compare_fusion.13, pred[512,32,512]{2,1,0:T(32,128)(4,1)} %iota_compare_fusion.14, bf16[96,4]{0,1:T(4,128)(2,1)S(1)} %get-tuple-element.520), kind=kOutput, calls=%fused_computation.1.clone.1 | convolution fusion | flops 251658240 | bytes 29360896 | tf_op jit(solution)/shard_map/while/body/eval_jaxpr/ibj,bh->hij/dot_general | solution.py:36
  229.6 17.5 %fusion.146 = f32[512,512,4]{1,2,0:T(4,128)} fusion(pred[512,32,512]{2,1,0:T(32,128)(4,1)} %iota_compare_fusion.12, pred[512,32,512]{2,1,0:T(32,128)(4,1)} %iota_compare_fusion.13, pred[512,32,512]{2,1,0:T(32,128)(4,1)} %iota_compare_fusion.14, bf16[96,4]{0,1:T(4,128)(2,1)S(1)} %get-tuple-element.520), kind=kOutput, calls=%fused_computation.1.clone.1 | convolution fusion | flops 251658240 | bytes 29360896 | tf_op jit(solution)/shard_map/while/body/eval_jaxpr/ibj,bh->hij/dot_general | solution.py:36
  290.3 17.5 %fusion.146 = f32[512,512,4]{1,2,0:T(4,128)} fusion(pred[512,32,512]{2,1,0:T(32,128)(4,1)} %iota_compare_fusion.12, pred[512,32,512]{2,1,0:T(32,128)(4,1)} %iota_compare_fusion.13, pred[512,32,512]{2,1,0:T(32,128)(4,1)} %iota_compare_fusion.14, bf16[96,4]{0,1:T(4,128)(2,1)S(1)} %get-tuple-element.520), kind=kOutput, calls=%fused_computation.1.clone.1 | convolution fusion | flops 251658240 | bytes 29360896 | tf_op jit(solution)/shard_map/while/body/eval_jaxpr/ibj,bh->hij/dot_general | solution.py:36
  328.9 71.2 %reduce-scatter.20.cloned.1.call-done = f32[512,1024]{1,0:T(8,128)} async-done(((f32[2048,1024]{1,0:T(8,128)}), f32[512,1024]{1,0:T(8,128)}) %reduce-scatter.20.cloned.1.call-update) | async-done | bytes 2097168 | tf_op jit(solution)/shard_map/reduce_scatter | solution.py:146
  404.4 34.0 %all-gather.7.cloned.1.call-done = bf16[2048,1024]{1,0:T(8,128)(2,1)} async-done(((bf16[512,1024]{1,0:T(8,128)(2,1)}), bf16[2048,1024]{1,0:T(8,128)(2,1)}) %all-gather.7.cloned.1.call-update) | async-done | bytes 4194320 | tf_op jit(solution)/shard_map/all_gather | solution.py:154
  452.1 22.3 %all-gather.9.cloned.1.call-done = bf16[2048,1024]{1,0:T(8,128)(2,1)} async-done(((bf16[512,1024]{1,0:T(8,128)(2,1)}), bf16[2048,1024]{1,0:T(8,128)(2,1)}) %all-gather.9.cloned.1.call-update) | async-done | bytes 4194320 | tf_op jit(solution)/shard_map/all_gather | solution.py:166
  496.3 71.8 %reduce-scatter.24.cloned.1.call-done = f32[512,1024]{1,0:T(8,128)} async-done(((f32[2048,1024]{1,0:T(8,128)}), f32[512,1024]{1,0:T(8,128)}) %reduce-scatter.24.cloned.1.call-update) | async-done | bytes 2097168 | tf_op jit(solution)/shard_map/reduce_scatter | solution.py:176
  621.3 447.7 %while.29 = (s32[]{:T(128)}, bf16[4,512,4,64]{1,3,2,0:T(8,128)(2,1)}, bf16[4,512,4,64]{1,3,2,0:T(8,128)(2,1)}, bf16[4,512,4,64]{1,3,2,0:T(8,128)(2,1)}, f32[4,96...) while((s32[]{:T(128)}, ...), condition=%wide.region_12.13_spmd, body=%wide.region_10.12_spmd.sunk | while | flops 1159067648 | bytes 209244656 | solution.py:192
  673.7 17.6 %pad_add_fusion.7 = pred[512,96,512]{2,1,0:T(32,128)(4,1)} fusion(pred[512,32,512]{2,1,0:T(32,128)(4,1)} %iota_compare_fusion.15, pred[512,32,512]{2,1,0:T(32,128)(4,1)} %iota_compare_fusion.16, pred[512,32,512]{2,1,0:T(32,128)(4,1)} %iota_compare_fusion.17), kind=kLoop, calls=%fused_computation.29.clone.1 | loop fusion | flops 50331648 | bytes 50331648 | tf_op jit(solution)/shard_map/while/body/eval_jaxpr/concatenate | solution.py:31
  729.3 16.9 %fusion.167 = f32[4,96,4]{1,2,0:T(4,128)} fusion(f32[4,96,4]{1,2,0:T(4,128)} %get-tuple-element.542, s32[]{:T(128)S(6)} %copy.127, pred[512,96,512]{2,1,0:T(32,128)(4,1)} %pad_add_fusion.7, bf16[4,512,512]{2,0,1:T(4,128)(2,1)} %copy.104), kind=kOutput, calls=%fused_computation.51.clone.1 | convolution fusion | flops 201326592 | bytes 27265028 | tf_op jit(solution)/shard_map/while/body/eval_jaxpr/ibj,hij->bh/dot_general | solution.py:82
  781.5 17.7 %pad_add_fusion.7 = pred[512,96,512]{2,1,0:T(32,128)(4,1)} fusion(pred[512,32,512]{2,1,0:T(32,128)(4,1)} %iota_compare_fusion.15, pred[512,32,512]{2,1,0:T(32,128)(4,1)} %iota_compare_fusion.16, pred[512,32,512]{2,1,0:T(32,128)(4,1)} %iota_compare_fusion.17), kind=kLoop, calls=%fused_computation.29.clone.1 | loop fusion | flops 50331648 | bytes 50331648 | tf_op jit(solution)/shard_map/while/body/eval_jaxpr/concatenate | solution.py:31
  837.1 16.7 %fusion.167 = f32[4,96,4]{1,2,0:T(4,128)} fusion(f32[4,96,4]{1,2,0:T(4,128)} %get-tuple-element.542, s32[]{:T(128)S(6)} %copy.127, pred[512,96,512]{2,1,0:T(32,128)(4,1)} %pad_add_fusion.7, bf16[4,512,512]{2,0,1:T(4,128)(2,1)} %copy.104), kind=kOutput, calls=%fused_computation.51.clone.1 | convolution fusion | flops 201326592 | bytes 27265028 | tf_op jit(solution)/shard_map/while/body/eval_jaxpr/ibj,hij->bh/dot_general | solution.py:82
  889.1 17.5 %pad_add_fusion.7 = pred[512,96,512]{2,1,0:T(32,128)(4,1)} fusion(pred[512,32,512]{2,1,0:T(32,128)(4,1)} %iota_compare_fusion.15, pred[512,32,512]{2,1,0:T(32,128)(4,1)} %iota_compare_fusion.16, pred[512,32,512]{2,1,0:T(32,128)(4,1)} %iota_compare_fusion.17), kind=kLoop, calls=%fused_computation.29.clone.1 | loop fusion | flops 50331648 | bytes 50331648 | tf_op jit(solution)/shard_map/while/body/eval_jaxpr/concatenate | solution.py:31
  944.5 16.7 %fusion.167 = f32[4,96,4]{1,2,0:T(4,128)} fusion(f32[4,96,4]{1,2,0:T(4,128)} %get-tuple-element.542, s32[]{:T(128)S(6)} %copy.127, pred[512,96,512]{2,1,0:T(32,128)(4,1)} %pad_add_fusion.7, bf16[4,512,512]{2,0,1:T(4,128)(2,1)} %copy.104), kind=kOutput, calls=%fused_computation.51.clone.1 | convolution fusion | flops 201326592 | bytes 27265028 | tf_op jit(solution)/shard_map/while/body/eval_jaxpr/ibj,hij->bh/dot_general | solution.py:82
  996.6 17.5 %pad_add_fusion.7 = pred[512,96,512]{2,1,0:T(32,128)(4,1)} fusion(pred[512,32,512]{2,1,0:T(32,128)(4,1)} %iota_compare_fusion.15, pred[512,32,512]{2,1,0:T(32,128)(4,1)} %iota_compare_fusion.16, pred[512,32,512]{2,1,0:T(32,128)(4,1)} %iota_compare_fusion.17), kind=kLoop, calls=%fused_computation.29.clone.1 | loop fusion | flops 50331648 | bytes 50331648 | tf_op jit(solution)/shard_map/while/body/eval_jaxpr/concatenate | solution.py:31
  1124.5 38.4 %all-reduce.6 = (bf16[32,4]{1,0:T(8,128)(2,1)}, bf16[32,4]{1,0:T(8,128)(2,1)}, bf16[32,4]{1,0:T(8,128)(2,1)}) all-reduce(bf16[32,4]{1,0:T(8,128)(2,1)} %copy.80, bf16[32,4]{1,0:T(8,128)(2,1)} %copy.81, bf16[32,4]{1,0:T(8,128)(2,1)} %copy.82), channel_id=12, replica_groups=mesh['wide'=8,'narrow'=4] {'wide'}, use_global_device_ids=true, to_apply=%region_24.25.clone | all-reduce | flops 384 | bytes 1536
  1169.8 37.6 %reduce-scatter.28.cloned.1.call-done = bf16[128,256]{1,0:T(8,128)(2,1)} async-done(((bf16[1024,256]{1,0:T(8,128)(2,1)}), bf16[128,256]{1,0:T(8,128)(2,1)}) %reduce-scatter.28.cloned.1.call-update) | async-done | bytes 65552 | tf_op jit(solution)/shard_map/reduce_scatter | solution.py:220
  1208.8 63.0 %reduce-scatter.30.cloned.1.call-done = bf16[128,256]{1,0:T(8,128)(2,1)} async-done(((bf16[1024,256]{1,0:T(8,128)(2,1)}), bf16[128,256]{1,0:T(8,128)(2,1)}) %reduce-scatter.30.cloned.1.call-update) | async-done | bytes 65552 | tf_op jit(solution)/shard_map/reduce_scatter | solution.py:226
  1273.3 63.3 %reduce-scatter.32.cloned.1.call-done = bf16[128,256]{1,0:T(8,128)(2,1)} async-done(((bf16[1024,256]{1,0:T(8,128)(2,1)}), bf16[128,256]{1,0:T(8,128)(2,1)}) %reduce-scatter.32.cloned.1.call-update) | async-done | bytes 65552 | tf_op jit(solution)/shard_map/reduce_scatter | solution.py:232
  1338.1 44.7 %reduce-scatter.26.cloned.1.call-done = bf16[512,1024]{1,0:T(8,128)(2,1)} async-done(((bf16[2048,1024]{1,0:T(8,128)(2,1)}), bf16[512,1024]{1,0:T(8,128)(2,1)}) %reduce-scatter.26.cloned.1.call-update) | async-done | bytes 1048592 | tf_op jit(solution)/shard_map/reduce_scatter | solution.py:211
  1385.8 39.9 %all-reduce.5 = (f32[1024]{0:T(1024)}, f32[1024]{0:T(1024)}) all-reduce(f32[1024]{0:T(1024)} %get-tuple-element.227, f32[1024]{0:T(1024)} %get-tuple-element.225), channel_id=6, replica_groups=mesh['wide'=8,'narrow'=4] {'wide','narrow'}, use_global_device_ids=true, to_apply=%region_16.17.clone | all-reduce | flops 2048 | bytes 16384
  (312 shorter events, 697.2 us)
Async XLA Ops:
  7.2 467.2 %copy-start = (bf16[704,1024]{1,0:T(8,128)(2,1)S(1)}, bf16[704,1024]{1,0:T(8,128)(2,1)}, u32[]{:S(2)}) copy-start(bf16[704,1024]{1,0:T(8,128)(2,1)} %param.36) | copy-start | bytes 4325380
  7.3 42.9 %all-gather.5.cloned.1.call-start = ((), (), s32[]{:S(2)}) async-start(), calls=%async_computation.11 | async-start | bytes 5242880 | tf_op jit(solution)/shard_map/all_gather | solution.py:133
  12.8 387.3 %reduce-scatter.20.cloned.1.call-start = ((), (), s32[]{:S(2)}) async-start(), calls=%async_computation.12 | async-start | bytes 10485760 | tf_op jit(solution)/shard_map/reduce_scatter | solution.py:146
  328.2 110.2 %all-gather.7.cloned.1.call-start = ((), (), s32[]{:S(2)}) async-start(), calls=%async_computation.13 | async-start | bytes 5242880 | tf_op jit(solution)/shard_map/all_gather | solution.py:154
  328.9 242.1 %copy-start.13 = (f32[1024]{0:T(1024)}, f32[1024]{0:T(1024)S(1)}, u32[]{:S(2)}) copy-start(f32[1024]{0:T(1024)S(1)} %convert_element_type.142) | copy-start | bytes 12292
  402.3 168.7 %copy-start.2 = (f32[512,1024]{1,0:T(8,128)}, f32[512,1024]{1,0:T(8,128)S(1)}, u32[]{:S(2)}) copy-start(f32[512,1024]{1,0:T(8,128)S(1)} %get-tuple-element.287) | copy-start | bytes 6291460
  402.3 168.7 %copy-start.17 = (f32[512]{0:T(512)}, f32[512]{0:T(512)S(1)}, u32[]{:S(2)}) copy-start(f32[512]{0:T(512)S(1)} %add_rsqrt_fusion) | copy-start | bytes 6148
  403.8 70.6 %all-gather.9.cloned.1.call-start = ((), (), s32[]{:S(2)}) async-start(), calls=%async_computation.15 | async-start | bytes 5242880 | tf_op jit(solution)/shard_map/all_gather | solution.py:166
  404.4 163.8 %reduce-scatter.24.cloned.1.call-start = ((), (), s32[]{:S(2)}) async-start(), calls=%async_computation.16 | async-start | bytes 10485760 | tf_op jit(solution)/shard_map/reduce_scatter | solution.py:176
  496.3 111.7 %all-gather.11.cloned.1.call-start = ((), (), s32[]{:S(2)}) async-start(), calls=%async_computation.17 | async-start | bytes 5242880 | tf_op jit(solution)/shard_map/all_gather | solution.py:186
  573.3 534.1 %reduce-scatter.40.cloned.1.call-start = ((), (), s32[]{:S(2)}) async-start(), calls=%async_computation.25 | async-start | bytes 1769472
  581.6 529.2 %reduce-scatter.38.cloned.1.call-start = ((), (), s32[]{:S(2)}) async-start(), calls=%async_computation.24 | async-start | bytes 1769472
  590.0 524.2 %reduce-scatter.36.cloned.1.call-start = ((), (), s32[]{:S(2)}) async-start(), calls=%async_computation.23 | async-start | bytes 1769472
  597.9 568.8 %reduce-scatter.34.cloned.1.call-start = ((), (), s32[]{:S(2)}) async-start(), calls=%async_computation.22 | async-start | bytes 589824
  1080.9 126.4 %reduce-scatter.28.cloned.1.call-start = ((), (), s32[]{:S(2)}) async-start(), calls=%async_computation.19 | async-start | bytes 589824 | tf_op jit(solution)/shard_map/reduce_scatter | solution.py:220
  1088.8 183.0 %reduce-scatter.30.cloned.1.call-start = ((), (), s32[]{:S(2)}) async-start(), calls=%async_computation.20 | async-start | bytes 589824 | tf_op jit(solution)/shard_map/reduce_scatter | solution.py:226
  1089.4 247.2 %reduce-scatter.32.cloned.1.call-start = ((), (), s32[]{:S(2)}) async-start(), calls=%async_computation.21 | async-start | bytes 589824 | tf_op jit(solution)/shard_map/reduce_scatter | solution.py:232
  1090.2 292.7 %reduce-scatter.26.cloned.1.call-start = ((), (), s32[]{:S(2)}) async-start(), calls=%async_computation.18 | async-start | bytes 5242880 | tf_op jit(solution)/shard_map/reduce_scatter | solution.py:211
  1098.3 332.2 %reduce-scatter.22.cloned.1.call-start = ((), (), s32[]{:S(2)}) async-start(), calls=%async_computation.14 | async-start | bytes 5242880 | tf_op jit(solution)/shard_map/reduce_scatter | solution.py:158
  1105.3 277.5 %copy-start.16 = (f32[1024]{0:T(1024)S(1)}, f32[1024]{0:T(1024)}, u32[]{:S(2)}) copy-start(f32[1024]{0:T(1024)} %copy-done.15) | copy-start | bytes 12292
  1105.3 277.5 %copy-start.22 = (f32[512]{0:T(512)S(1)}, f32[512]{0:T(512)}, u32[]{:S(2)}) copy-start(f32[512]{0:T(512)} %copy-done.21) | copy-start | bytes 6148
  1105.3 325.1 %copy-start.3 = (f32[512,1024]{1,0:T(8,128)S(1)}, f32[512,1024]{1,0:T(8,128)}, u32[]{:S(2)}) copy-start(f32[512,1024]{1,0:T(8,128)} %copy-done.2) | copy-start | bytes 6291460
  1105.3 325.1 %copy-start.14 = (f32[1024]{0:T(1024)S(1)}, f32[1024]{0:T(1024)}, u32[]{:S(2)}) copy-start(f32[1024]{0:T(1024)} %copy-done.13) | copy-start | bytes 12292
  1105.3 325.1 %copy-start.18 = (f32[512]{0:T(512)S(1)}, f32[512]{0:T(512)}, u32[]{:S(2)}) copy-start(f32[512]{0:T(512)} %copy-done.17) | copy-start | bytes 6148
  (33 other events, 218.6 us)
Sparse Core Ops, SparseCore 0:
  12.9 37.1 all-gather.4
  328.3 71.7 reduce-scatter.19
  403.9 34.4 all-gather.6
  439.9 34.4 all-gather.8
  496.4 71.6 reduce-scatter.23
  573.4 34.4 all-gather.10
  611.3 64.8 reduce-scatter.39
  680.0 63.7 reduce-scatter.37
  747.3 63.6 reduce-scatter.35
  1081.0 61.9 reduce-scatter.33
  1146.3 60.9 reduce-scatter.27
  1210.9 60.8 reduce-scatter.29
  1275.7 60.8 reduce-scatter.31
  1339.2 43.5 reduce-scatter.25
  1385.2 45.1 reduce-scatter.21
where the time goes:
time: 1450 us; the launch traced here: 1440 us
  waiting for transfers between devices  455 us (31%)
  matrix products  386 us (27%)
  other arithmetic  335 us (23%)
  local copies, waits for them, and re-layouts  153 us (11%)
  blocking collectives  78.3 us (5%)
  loops' own time  18.1 us (1%)
  between operations  15.2 us (1%)
    eq x24, other arithmetic, bucket_onehot(): bucket_ids[:, None, :] == levels  215 us
    dot_general x8, matrix products, page_scores(): jnp.einsum('ibj,bh->hij', one_hot, table_all, preferred_element_type=jnp....  134 us
    unnamed x2, blocking collectives  78.3 us
    reduce_scatter x1, waiting for transfers between devices, shards(): lax.psum_scatter(first + jnp.dot(grad_upper, wi_up.T, preferred_element_t...  71.8 us
    reduce_scatter x1, waiting for transfers between devices, shards(): lax.psum_scatter(jnp.dot(context_flat, w_output, preferred_element_type=j...  71.2 us
    concatenate x4, other arithmetic, bucket_onehot(): return jnp.concatenate(pieces, axis=1)  70.4 us
    dot_general x4, matrix products, page_backward(): jnp.einsum('ibj,hij->bh', one_hot, grad_low, preferred_element_type=jnp.f...  67 us
    reduce_scatter x1, waiting for transfers between devices, shards(): lax.psum_scatter(grad_w_joined[:, 2 * local_width:].astype(jnp.bfloat16),...  63.3 us
  transfers between devices with their start and end apart: 15, of which 11 were waited for; matrix products, arithmetic and copies ran while one was open for 38% of the time, Pallas kernels for 0%

commit v1 on v0

--- a/solution.py
+++ b/solution.py
@@ -130,7 +130,24 @@
     gain_second = gain_ffn.astype(jnp.float32)
     resid = hidden_in.astype(jnp.float32)
     normed, inv_first = rms_forward(resid, gain_first)
-    normed_all = lax.all_gather(normed.astype(jnp.bfloat16), "narrow", axis=0, tiled=True)
+    x = normed.astype(jnp.bfloat16)
+    length, position, span = (lax.axis_size("narrow"), lax.axis_index("narrow"), x.shape[0])
+    right = [(i, (i + 1) % length) for i in range(length)]
+    behind = [(i, (i - 1) % length) for i in range(length)]
+    normed_all = jnp.zeros((*x.shape[:0], length * span, *x.shape[0 + 1 :]), x.dtype)
+    normed_all = lax.dynamic_update_slice_in_dim(normed_all, x, position * span, axis=0)
+    from_left = from_right = x
+    halfway = length // 2
+    for step in range(1, halfway + 1):
+        from_left = lax.ppermute(from_left, "narrow", right)
+        normed_all = lax.dynamic_update_slice_in_dim(
+            normed_all, from_left, (position - step) % length * span, axis=0
+        )
+        if step < length - halfway:
+            from_right = lax.ppermute(from_right, "narrow", behind)
+            normed_all = lax.dynamic_update_slice_in_dim(
+                normed_all, from_right, (position + step) % length * span, axis=0
+            )
     projected = jnp.dot(normed_all, w_joined, preferred_element_type=jnp.float32).astype(
         jnp.bfloat16
     )

time: 1450 us -> 1480 us (1.021)
  loops' own time: 18.1 us -> 38.6 us
    all_gather x1 -> x0, waiting for transfers between devices: 34.4 us -> none  [shards(): lax.all_gather(normed.astype(jnp.bfloat16), 'narrow', axis=0, tiled=True)]
    ppermute x0 -> x3, waiting for transfers between devices: none -> 25.8 us  [the longest x2 25.8 us: shards(): from_left = lax.ppermute(from_left, 'narrow', right)]
  transfers between devices with their start and end apart: 15 -> 17, of which waited for: 11 -> 12; matrix products, arithmetic and copies ran while one was open for 38% -> 38% of each run, Pallas kernels for 0% -> 0%
where the time goes in v1:
time: 1480 us; the launch traced here: 1470 us
  waiting for transfers between devices  451 us (30%)
  matrix products  385 us (26%)
  other arithmetic  335 us (23%)
  local copies, waits for them, and re-layouts  159 us (11%)
  blocking collectives  78.4 us (5%)
  loops' own time  38.6 us (3%)
  between operations  15.2 us (1%)
    eq x24, other arithmetic, bucket_onehot(): bucket_ids[:, None, :] == levels  215 us
    dot_general x8, matrix products, page_scores(): jnp.einsum('ibj,bh->hij', one_hot, table_all, preferred_element_type=jnp....  134 us
    unnamed x2, blocking collectives  78.4 us
    reduce_scatter x1, waiting for transfers between devices, shards(): lax.psum_scatter(jnp.dot(context_flat, w_output, preferred_element_type=j...  75.2 us
    reduce_scatter x1, waiting for transfers between devices, shards(): lax.psum_scatter(first + jnp.dot(grad_upper, wi_up.T, preferred_element_t...  71.8 us
    concatenate x4, other arithmetic, bucket_onehot(): return jnp.concatenate(pieces, axis=1)  70.6 us
    dot_general x4, matrix products, page_backward(): jnp.einsum('ibj,hij->bh', one_hot, grad_low, preferred_element_type=jnp.f...  67 us
    reduce_scatter x1, waiting for transfers between devices, shards(): lax.psum_scatter(grad_w_joined[:, 2 * local_width:].astype(jnp.bfloat16),...  63.2 us
  transfers between devices with their start and end apart: 17, of which 12 were waited for; matrix products, arithmetic and copies ran while one was open for 38% of the time, Pallas kernels for 0%

profile of v1, /device:TPU:0, one launch (start us, length us, event | category | flops | bytes accessed | tf_op | source)
XLA Modules:
  0.0 1468.8 jit_solution(17675420270767965088)
XLA Ops:
  15.9 21.2 %collective-permute-done = bf16[512,1024]{1,0:T(8,128)(2,1)S(1)} collective-permute-done((bf16[512,1024]{1,0:T(8,128)(2,1)}, bf16[512,1024]{1,0:T(8,128)(2,1)S(1)}, u32[]{:S(2)}, u32[]{:S(2)}) %collective-permute-start) | collective-permute-done | bytes 1048608 | tf_op jit(solution)/shard_map/ppermute | solution.py:142
  78.4 256.5 %while.28 = (s32[]{:T(128)}, bf16[4,512,4,64]{1,3,2,0:T(8,128)(2,1)}, f32[4,4,512]{2,1,0:T(4,128)}, bf16[4,512,4,64]{1,3,2,0:T(8,128)(2,1)}, pred[4,512]{1,0:T(4...) while((s32[]{:T(128)}, ...), condition=%wide.region_4.5_spmd, body=%wide.region_1.4_spmd.sunk | while | flops 553777152 | bytes 90247560 | solution.py:158
  122.5 17.5 %fusion.147 = f32[512,512,4]{1,2,0:T(4,128)} fusion(pred[512,32,512]{2,1,0:T(32,128)(4,1)} %iota_compare_fusion.12, pred[512,32,512]{2,1,0:T(32,128)(4,1)} %iota_compare_fusion.13, pred[512,32,512]{2,1,0:T(32,128)(4,1)} %iota_compare_fusion.14, bf16[96,4]{0,1:T(4,128)(2,1)S(1)} %get-tuple-element.522), kind=kOutput, calls=%fused_computation.1.clone.1 | convolution fusion | flops 251658240 | bytes 29360896 | tf_op jit(solution)/shard_map/while/body/eval_jaxpr/ibj,bh->hij/dot_general | solution.py:36
  183.2 17.5 %fusion.147 = f32[512,512,4]{1,2,0:T(4,128)} fusion(pred[512,32,512]{2,1,0:T(32,128)(4,1)} %iota_compare_fusion.12, pred[512,32,512]{2,1,0:T(32,128)(4,1)} %iota_compare_fusion.13, pred[512,32,512]{2,1,0:T(32,128)(4,1)} %iota_compare_fusion.14, bf16[96,4]{0,1:T(4,128)(2,1)S(1)} %get-tuple-element.522), kind=kOutput, calls=%fused_computation.1.clone.1 | convolution fusion | flops 251658240 | bytes 29360896 | tf_op jit(solution)/shard_map/while/body/eval_jaxpr/ibj,bh->hij/dot_general | solution.py:36
  243.9 17.5 %fusion.147 = f32[512,512,4]{1,2,0:T(4,128)} fusion(pred[512,32,512]{2,1,0:T(32,128)(4,1)} %iota_compare_fusion.12, pred[512,32,512]{2,1,0:T(32,128)(4,1)} %iota_compare_fusion.13, pred[512,32,512]{2,1,0:T(32,128)(4,1)} %iota_compare_fusion.14, bf16[96,4]{0,1:T(4,128)(2,1)S(1)} %get-tuple-element.522), kind=kOutput, calls=%fused_computation.1.clone.1 | convolution fusion | flops 251658240 | bytes 29360896 | tf_op jit(solution)/shard_map/while/body/eval_jaxpr/ibj,bh->hij/dot_general | solution.py:36
  304.7 17.5 %fusion.147 = f32[512,512,4]{1,2,0:T(4,128)} fusion(pred[512,32,512]{2,1,0:T(32,128)(4,1)} %iota_compare_fusion.12, pred[512,32,512]{2,1,0:T(32,128)(4,1)} %iota_compare_fusion.13, pred[512,32,512]{2,1,0:T(32,128)(4,1)} %iota_compare_fusion.14, bf16[96,4]{0,1:T(4,128)(2,1)S(1)} %get-tuple-element.522), kind=kOutput, calls=%fused_computation.1.clone.1 | convolution fusion | flops 251658240 | bytes 29360896 | tf_op jit(solution)/shard_map/while/body/eval_jaxpr/ibj,bh->hij/dot_general | solution.py:36
  343.5 75.2 %reduce-scatter.20.cloned.1.call-done = f32[512,1024]{1,0:T(8,128)} async-done(((f32[2048,1024]{1,0:T(8,128)}), f32[512,1024]{1,0:T(8,128)}) %reduce-scatter.20.cloned.1.call-update) | async-done | bytes 2097168 | tf_op jit(solution)/shard_map/reduce_scatter | solution.py:163
  423.1 33.8 %all-gather.4.cloned.1.call-done = bf16[2048,1024]{1,0:T(8,128)(2,1)} async-done(((bf16[512,1024]{1,0:T(8,128)(2,1)}), bf16[2048,1024]{1,0:T(8,128)(2,1)}) %all-gather.4.cloned.1.call-update) | async-done | bytes 4194320 | tf_op jit(solution)/shard_map/all_gather | solution.py:171
  470.7 22.4 %all-gather.6.cloned.1.call-done = bf16[2048,1024]{1,0:T(8,128)(2,1)} async-done(((bf16[512,1024]{1,0:T(8,128)(2,1)}), bf16[2048,1024]{1,0:T(8,128)(2,1)}) %all-gather.6.cloned.1.call-update) | async-done | bytes 4194320 | tf_op jit(solution)/shard_map/all_gather | solution.py:183
  515.0 71.8 %reduce-scatter.24.cloned.1.call-done = f32[512,1024]{1,0:T(8,128)} async-done(((f32[2048,1024]{1,0:T(8,128)}), f32[512,1024]{1,0:T(8,128)}) %reduce-scatter.24.cloned.1.call-update) | async-done | bytes 2097168 | tf_op jit(solution)/shard_map/reduce_scatter | solution.py:193
  640.1 455.9 %while.29 = (s32[]{:T(128)}, bf16[4,512,4,64]{1,3,2,0:T(8,128)(2,1)}, bf16[4,512,4,64]{1,3,2,0:T(8,128)(2,1)}, bf16[4,512,4,64]{1,3,2,0:T(8,128)(2,1)}, f32[4,96...) while((s32[]{:T(128)}, ...), condition=%wide.region_12.13_spmd, body=%wide.region_10.12_spmd.sunk | while | flops 1159067648 | bytes 209244656 | solution.py:209
  692.5 17.7 %pad_add_fusion.7 = pred[512,96,512]{2,1,0:T(32,128)(4,1)} fusion(pred[512,32,512]{2,1,0:T(32,128)(4,1)} %iota_compare_fusion.15, pred[512,32,512]{2,1,0:T(32,128)(4,1)} %iota_compare_fusion.16, pred[512,32,512]{2,1,0:T(32,128)(4,1)} %iota_compare_fusion.17), kind=kLoop, calls=%fused_computation.29.clone.1 | loop fusion | flops 50331648 | bytes 50331648 | tf_op jit(solution)/shard_map/while/body/eval_jaxpr/concatenate | solution.py:31
  748.2 16.8 %fusion.168 = f32[4,96,4]{1,2,0:T(4,128)} fusion(f32[4,96,4]{1,2,0:T(4,128)} %get-tuple-element.544, s32[]{:T(128)S(6)} %copy.131, pred[512,96,512]{2,1,0:T(32,128)(4,1)} %pad_add_fusion.7, bf16[4,512,512]{2,0,1:T(4,128)(2,1)} %copy.104), kind=kOutput, calls=%fused_computation.51.clone.1 | convolution fusion | flops 201326592 | bytes 27265028 | tf_op jit(solution)/shard_map/while/body/eval_jaxpr/ibj,hij->bh/dot_general | solution.py:82
  800.5 17.8 %pad_add_fusion.7 = pred[512,96,512]{2,1,0:T(32,128)(4,1)} fusion(pred[512,32,512]{2,1,0:T(32,128)(4,1)} %iota_compare_fusion.15, pred[512,32,512]{2,1,0:T(32,128)(4,1)} %iota_compare_fusion.16, pred[512,32,512]{2,1,0:T(32,128)(4,1)} %iota_compare_fusion.17), kind=kLoop, calls=%fused_computation.29.clone.1 | loop fusion | flops 50331648 | bytes 50331648 | tf_op jit(solution)/shard_map/while/body/eval_jaxpr/concatenate | solution.py:31
  856.2 16.7 %fusion.168 = f32[4,96,4]{1,2,0:T(4,128)} fusion(f32[4,96,4]{1,2,0:T(4,128)} %get-tuple-element.544, s32[]{:T(128)S(6)} %copy.131, pred[512,96,512]{2,1,0:T(32,128)(4,1)} %pad_add_fusion.7, bf16[4,512,512]{2,0,1:T(4,128)(2,1)} %copy.104), kind=kOutput, calls=%fused_computation.51.clone.1 | convolution fusion | flops 201326592 | bytes 27265028 | tf_op jit(solution)/shard_map/while/body/eval_jaxpr/ibj,hij->bh/dot_general | solution.py:82
  908.4 17.5 %pad_add_fusion.7 = pred[512,96,512]{2,1,0:T(32,128)(4,1)} fusion(pred[512,32,512]{2,1,0:T(32,128)(4,1)} %iota_compare_fusion.15, pred[512,32,512]{2,1,0:T(32,128)(4,1)} %iota_compare_fusion.16, pred[512,32,512]{2,1,0:T(32,128)(4,1)} %iota_compare_fusion.17), kind=kLoop, calls=%fused_computation.29.clone.1 | loop fusion | flops 50331648 | bytes 50331648 | tf_op jit(solution)/shard_map/while/body/eval_jaxpr/concatenate | solution.py:31
  1015.9 17.5 %pad_add_fusion.7 = pred[512,96,512]{2,1,0:T(32,128)(4,1)} fusion(pred[512,32,512]{2,1,0:T(32,128)(4,1)} %iota_compare_fusion.15, pred[512,32,512]{2,1,0:T(32,128)(4,1)} %iota_compare_fusion.16, pred[512,32,512]{2,1,0:T(32,128)(4,1)} %iota_compare_fusion.17), kind=kLoop, calls=%fused_computation.29.clone.1 | loop fusion | flops 50331648 | bytes 50331648 | tf_op jit(solution)/shard_map/while/body/eval_jaxpr/concatenate | solution.py:31
  1071.4 16.7 %fusion.168 = f32[4,96,4]{1,2,0:T(4,128)} fusion(f32[4,96,4]{1,2,0:T(4,128)} %get-tuple-element.544, s32[]{:T(128)S(6)} %copy.131, pred[512,96,512]{2,1,0:T(32,128)(4,1)} %pad_add_fusion.7, bf16[4,512,512]{2,0,1:T(4,128)(2,1)} %copy.104), kind=kOutput, calls=%fused_computation.51.clone.1 | convolution fusion | flops 201326592 | bytes 27265028 | tf_op jit(solution)/shard_map/while/body/eval_jaxpr/ibj,hij->bh/dot_general | solution.py:82
  1150.7 38.5 %all-reduce.6 = (bf16[32,4]{1,0:T(8,128)(2,1)}, bf16[32,4]{1,0:T(8,128)(2,1)}, bf16[32,4]{1,0:T(8,128)(2,1)}) all-reduce(bf16[32,4]{1,0:T(8,128)(2,1)} %copy.80, bf16[32,4]{1,0:T(8,128)(2,1)} %copy.81, bf16[32,4]{1,0:T(8,128)(2,1)} %copy.82), channel_id=12, replica_groups=mesh['wide'=8,'narrow'=4] {'wide'}, use_global_device_ids=true, to_apply=%region_24.25.clone | all-reduce | flops 384 | bytes 1536
  1196.0 38.0 %reduce-scatter.28.cloned.1.call-done = bf16[128,256]{1,0:T(8,128)(2,1)} async-done(((bf16[1024,256]{1,0:T(8,128)(2,1)}), bf16[128,256]{1,0:T(8,128)(2,1)}) %reduce-scatter.28.cloned.1.call-update) | async-done | bytes 65552 | tf_op jit(solution)/shard_map/reduce_scatter | solution.py:237
  1235.5 63.1 %reduce-scatter.30.cloned.1.call-done = bf16[128,256]{1,0:T(8,128)(2,1)} async-done(((bf16[1024,256]{1,0:T(8,128)(2,1)}), bf16[128,256]{1,0:T(8,128)(2,1)}) %reduce-scatter.30.cloned.1.call-update) | async-done | bytes 65552 | tf_op jit(solution)/shard_map/reduce_scatter | solution.py:243
  1300.2 63.2 %reduce-scatter.32.cloned.1.call-done = bf16[128,256]{1,0:T(8,128)(2,1)} async-done(((bf16[1024,256]{1,0:T(8,128)(2,1)}), bf16[128,256]{1,0:T(8,128)(2,1)}) %reduce-scatter.32.cloned.1.call-update) | async-done | bytes 65552 | tf_op jit(solution)/shard_map/reduce_scatter | solution.py:249
  1364.9 44.7 %reduce-scatter.26.cloned.1.call-done = bf16[512,1024]{1,0:T(8,128)(2,1)} async-done(((bf16[2048,1024]{1,0:T(8,128)(2,1)}), bf16[512,1024]{1,0:T(8,128)(2,1)}) %reduce-scatter.26.cloned.1.call-update) | async-done | bytes 1048592 | tf_op jit(solution)/shard_map/reduce_scatter | solution.py:228
  1412.6 39.9 %all-reduce.5 = (f32[1024]{0:T(1024)}, f32[1024]{0:T(1024)}) all-reduce(f32[1024]{0:T(1024)} %get-tuple-element.227, f32[1024]{0:T(1024)} %get-tuple-element.225), channel_id=6, replica_groups=mesh['wide'=8,'narrow'=4] {'wide','narrow'}, use_global_device_ids=true, to_apply=%region_16.17.clone | all-reduce | flops 2048 | bytes 16384
  (315 shorter events, 712.1 us)
Async XLA Ops:
  7.2 486.0 %copy-start = (bf16[704,1024]{1,0:T(8,128)(2,1)S(1)}, bf16[704,1024]{1,0:T(8,128)(2,1)}, u32[]{:S(2)}) copy-start(bf16[704,1024]{1,0:T(8,128)(2,1)} %param.36) | copy-start | bytes 4325380
  7.2 411.5 %reduce-scatter.20.cloned.1.call-start = ((), (), s32[]{:S(2)}) async-start(), calls=%async_computation.11 | async-start | bytes 10485760 | tf_op jit(solution)/shard_map/reduce_scatter | solution.py:163
  13.4 23.7 %collective-permute-start = (bf16[512,1024]{1,0:T(8,128)(2,1)}, bf16[512,1024]{1,0:T(8,128)(2,1)S(1)}, u32[]{:S(2)}, u32[]{:S(2)}) collective-permute-start(bf16[512,1024]{1,0:T(8,128)(2,1)} %get-tuple-element.289), channel_id=1, source_target_pairs={{0,1},{1,2},{2,3},{3,0},{4,5},{5,6},{6,7},{7,4},{8,9},{9,10},{10,1... | collective-permute-start | bytes 3145736 | tf_op jit(solution)/shard_map/ppermute | solution.py:142
  13.9 31.8 %collective-permute-start.1 = (bf16[512,1024]{1,0:T(8,128)(2,1)}, bf16[512,1024]{1,0:T(8,128)(2,1)S(1)}, u32[]{:S(2)}, u32[]{:S(2)}) collective-permute-start(bf16[512,1024]{1,0:T(8,128)(2,1)} %get-tuple-element.289), channel_id=1, source_target_pairs={{0,3},{1,0},{2,1},{3,2},{4,7},{5,4},{6,5},{7,6},{8,11},{9,8},{10,9... | collective-permute-start | bytes 3145736 | tf_op jit(solution)/shard_map/ppermute | solution.py:147
  37.1 14.2 collective-permute-start.2
  342.9 114.1 %all-gather.4.cloned.1.call-start = ((), (), s32[]{:S(2)}) async-start(), calls=%async_computation.12 | async-start | bytes 5242880 | tf_op jit(solution)/shard_map/all_gather | solution.py:171
  343.5 246.2 %copy-start.14 = (f32[1024]{0:T(1024)}, f32[1024]{0:T(1024)S(1)}, u32[]{:S(2)}) copy-start(f32[1024]{0:T(1024)S(1)} %convert_element_type.142) | copy-start | bytes 12292
  422.4 70.8 %all-gather.6.cloned.1.call-start = ((), (), s32[]{:S(2)}) async-start(), calls=%async_computation.14 | async-start | bytes 5242880 | tf_op jit(solution)/shard_map/all_gather | solution.py:183
  423.1 163.8 %reduce-scatter.24.cloned.1.call-start = ((), (), s32[]{:S(2)}) async-start(), calls=%async_computation.15 | async-start | bytes 10485760 | tf_op jit(solution)/shard_map/reduce_scatter | solution.py:193
  515.0 111.7 %all-gather.8.cloned.1.call-start = ((), (), s32[]{:S(2)}) async-start(), calls=%async_computation.16 | async-start | bytes 5242880 | tf_op jit(solution)/shard_map/all_gather | solution.py:203
  592.0 541.6 %reduce-scatter.40.cloned.1.call-start = ((), (), s32[]{:S(2)}) async-start(), calls=%async_computation.24 | async-start | bytes 1769472
  600.2 536.8 %reduce-scatter.38.cloned.1.call-start = ((), (), s32[]{:S(2)}) async-start(), calls=%async_computation.23 | async-start | bytes 1769472
  608.7 531.8 %reduce-scatter.36.cloned.1.call-start = ((), (), s32[]{:S(2)}) async-start(), calls=%async_computation.22 | async-start | bytes 1769472
  616.6 576.3 %reduce-scatter.34.cloned.1.call-start = ((), (), s32[]{:S(2)}) async-start(), calls=%async_computation.21 | async-start | bytes 589824
  1107.9 126.2 %reduce-scatter.28.cloned.1.call-start = ((), (), s32[]{:S(2)}) async-start(), calls=%async_computation.18 | async-start | bytes 589824 | tf_op jit(solution)/shard_map/reduce_scatter | solution.py:237
  1115.8 182.9 %reduce-scatter.30.cloned.1.call-start = ((), (), s32[]{:S(2)}) async-start(), calls=%async_computation.19 | async-start | bytes 589824 | tf_op jit(solution)/shard_map/reduce_scatter | solution.py:243
  1116.6 246.8 %reduce-scatter.32.cloned.1.call-start = ((), (), s32[]{:S(2)}) async-start(), calls=%async_computation.20 | async-start | bytes 589824 | tf_op jit(solution)/shard_map/reduce_scatter | solution.py:249
  1117.1 292.5 %reduce-scatter.26.cloned.1.call-start = ((), (), s32[]{:S(2)}) async-start(), calls=%async_computation.17 | async-start | bytes 5242880 | tf_op jit(solution)/shard_map/reduce_scatter | solution.py:228
  1124.3 333.0 %reduce-scatter.22.cloned.1.call-start = ((), (), s32[]{:S(2)}) async-start(), calls=%async_computation.13 | async-start | bytes 5242880 | tf_op jit(solution)/shard_map/reduce_scatter | solution.py:175
  1131.5 278.1 %copy-start.17 = (f32[1024]{0:T(1024)S(1)}, f32[1024]{0:T(1024)}, u32[]{:S(2)}) copy-start(f32[1024]{0:T(1024)} %copy-done.16) | copy-start | bytes 12292
  1131.5 278.1 %copy-start.23 = (f32[512]{0:T(512)S(1)}, f32[512]{0:T(512)}, u32[]{:S(2)}) copy-start(f32[512]{0:T(512)} %copy-done.22) | copy-start | bytes 6148
  1131.5 325.8 %copy-start.3 = (f32[512,1024]{1,0:T(8,128)S(1)}, f32[512,1024]{1,0:T(8,128)}, u32[]{:S(2)}) copy-start(f32[512,1024]{1,0:T(8,128)} %copy-done.2) | copy-start | bytes 6291460
  1131.5 325.8 %copy-start.15 = (f32[1024]{0:T(1024)S(1)}, f32[1024]{0:T(1024)}, u32[]{:S(2)}) copy-start(f32[1024]{0:T(1024)} %copy-done.14) | copy-start | bytes 12292
  1131.5 325.8 %copy-start.19 = (f32[512]{0:T(512)S(1)}, f32[512]{0:T(512)}, u32[]{:S(2)}) copy-start(f32[512]{0:T(512)} %copy-done.18) | copy-start | bytes 6148
  (33 other events, 595.8 us)
Sparse Core Ops, SparseCore 0:
  343.0 75.6 reduce-scatter.19
  422.5 34.4 all-gather.3
  458.6 34.4 all-gather.5
  515.1 71.7 reduce-scatter.23
  592.1 34.4 all-gather.7
  629.9 64.8 reduce-scatter.39
  698.6 63.7 reduce-scatter.37
  765.9 63.8 reduce-scatter.35
  1108.0 61.8 reduce-scatter.33
  1173.1 60.8 reduce-scatter.27
  1237.7 60.8 reduce-scatter.29
  1302.5 60.8 reduce-scatter.31
  1366.1 43.5 reduce-scatter.25
  1412.0 45.2 reduce-scatter.21
